TPU v7x, 256 devices: a whole 4x4x8 slice. The times are simulated.
256 devices in a mesh: img: 16 (over y, z_hi, core), depth: 16 (over x, z_lo).
Axes of the slice: x: 4, y: 4, z: 8 (z_hi: 2, z_lo: 4; z = z_hi * 4 + z_lo), core: 2. Of those that a mesh axis runs over, the one named last changes fastest.
Arguments:
- counts: int32 [512, 1024, 512], P('depth', 'img'), may hold values from 0 to 5, as said below
Outputs:
- image: float32 [4, 1024, 512], P(None, ('img', 'depth'))
Inputs may be any that keep to these rules, and one draw needn't show every extreme that they name: `counts`: whole numbers of atoms.
All inputs are finite; a program needn't handle non-finite values.
Results may differ from a plain program's by a relative error of at most 0.0003.
Values sent between devices are 32-bit elements; how exact they have to be, the bound alone decides.
A program may use at most 64 MiB of HBM per device.

v0:
```python
import math

import jax
import jax.numpy as jnp
from jax import lax
from jax.sharding import PartitionSpec as P

gauss_taps = [
    math.exp(-offset * offset / 8.0)
    / sum((math.exp(-other * other / 8.0) for other in range(-4, 5)))
    for offset in range(-4, 5)
]
light_z = 0.48
light_x = 0.6
light_y = 0.64


def extended(block, sides, width):
    for axis, dim in sides:
        count = lax.axis_size(axis)
        forward = [(i, i + 1) for i in range(count - 1)]
        backward = [(target, source) for source, target in forward]
        low = lax.ppermute(
            lax.slice_in_dim(block, block.shape[dim] - width, None, axis=dim), axis, forward
        )
        high = lax.ppermute(lax.slice_in_dim(block, 0, width, axis=dim), axis, backward)
        block = jnp.concatenate([low, block, high], axis=dim)
    return block


def extended_2(shard, sides, width):
    edges = {}
    for axis, dim in sides:
        count, length = (lax.axis_size(axis), shard.shape[dim])
        up = [(i, (i + 1) % count) for i in range(count - 1)]
        last = lax.slice_in_dim(shard, length - width, length, axis=dim)
        leading = lax.slice_in_dim(shard, 0, width, axis=dim)
        edges[dim] = (
            lax.ppermute(last, axis, up),
            lax.ppermute(leading, axis, [(b, a) for a, b in up]),
        )
    done = []
    for _, dim in sides:
        low, high = edges[dim]
        around = [(width, width) if d in done else (0, 0) for d in range(shard.ndim)]
        shard = jnp.concatenate([jnp.pad(low, around), shard, jnp.pad(high, around)], axis=dim)
        done.append(dim)
    return shard


def smooth_valid(values, axis):
    length = values.shape[axis] - 8
    total = gauss_taps[0] * lax.slice_in_dim(values, 0, length, axis=axis)
    for offset in range(1, 9):
        total = total + gauss_taps[offset] * lax.slice_in_dim(
            values, offset, offset + length, axis=axis
        )
    return total


def smooth_last(values):
    widths = [(0, 0)] * (values.ndim - 1) + [(4, 4)]
    return smooth_valid(jnp.pad(values, widths), values.ndim - 1)


def render_terms(smooth_ext, depth_total):
    smoothed = smooth_ext[1:-1, 1:-1, :]
    grad_z = 0.5 * (smooth_ext[2:, 1:-1, :] - smooth_ext[:-2, 1:-1, :])
    grad_x = 0.5 * (smooth_ext[1:-1, 2:, :] - smooth_ext[1:-1, :-2, :])
    padded = jnp.pad(smoothed, ((0, 0), (0, 0), (1, 1)))
    grad_y = 0.5 * (padded[:, :, 2:] - padded[:, :, :-2])
    shading = 0.55 + 0.45 * jnp.tanh(3.0 * (light_z * grad_z + light_x * grad_x + light_y * grad_y))
    gradient_sq = grad_z * grad_z + grad_x * grad_x + grad_y * grad_y
    optical = (
        1.5
        / depth_total
        * smoothed
        * smoothed
        / (1.0 + smoothed * smoothed)
        * (1.0 + 4.0 * gradient_sq)
    )
    sigma_red = jax.nn.sigmoid(2.0 * (smoothed - 2.5))
    red_light = shading * sigma_red
    green_light = shading * jnp.exp(-((smoothed - 2.5) ** 2))
    blue_light = shading * (1.0 - sigma_red)
    return (optical, red_light, green_light, blue_light)


def integrate(optical, red_light, green_light, blue_light):
    before = jnp.cumsum(optical, axis=0) - optical
    weight = jnp.exp(-before) * (1.0 - jnp.exp(-optical))
    colors = jnp.stack(
        [
            jnp.sum(weight * red_light, 0),
            jnp.sum(weight * green_light, 0),
            jnp.sum(weight * blue_light, 0),
        ],
        0,
    )
    transmit = jnp.exp(-jnp.sum(optical, 0))
    return (colors, transmit)


def local(counts):
    density = smooth_last(counts.astype(jnp.float32))
    slab_depth, tile_rows, columns = density.shape
    depth_count = lax.axis_size("depth")
    depth_total = slab_depth * depth_count
    smooth_x = smooth_valid(extended(density, (("img", 1),), 4), 1)
    smoothed = smooth_valid(extended(smooth_x, (("depth", 0),), 4), 0)
    smooth_ext = extended_2(smoothed, (("depth", 0), ("img", 1)), 1)
    colors, transmit = integrate(*render_terms(smooth_ext, depth_total))
    layers = jnp.concatenate([colors, transmit[None]], 0)
    rows_owned = tile_rows // depth_count
    pieces = layers.reshape(4, depth_count, rows_owned, columns)
    arrived = lax.all_to_all(pieces, "depth", split_axis=1, concat_axis=1, tiled=True)
    running = jnp.cumprod(arrived[3], axis=0)
    exclusive = jnp.concatenate([jnp.ones_like(running[:1]), running[:-1]], 0)
    shaded = jnp.sum(exclusive[None] * arrived[:3], axis=1)
    result = jnp.concatenate([shaded, running[-1:]], 0)
    return jnp.concatenate([result[:3], 1.0 - result[3:]], 0)


def solution(mesh):
    in_specs = (P("depth", "img", None),)
    out_specs = P(None, ("img", "depth"), None)
    return jax.shard_map(local, mesh=mesh, in_specs=in_specs, out_specs=out_specs, check_vma=False)
```

profile of v0, /device:TPU:14, one launch (start us, length us, event | category | flops | bytes accessed | tf_op | source)
XLA Modules:
  0.0 147.0 jit_solution(10868958833424034168)
XLA Ops:
  0.0 4.9 %convert_element_type.10 = f32[32,64,512]{2,1,0:T(8,128)} convert(s32[32,64,512]{2,1,0:T(8,128)} %param.1) | non-fusion elementwise | flops 1048576 | bytes 8388608 | tf_op jit(solution)/shard_map/convert_element_type | solution.py:105
  4.9 22.1 %fusion.51 = f32[32,64,512]{2,1,0:T(8,128)S(1)} fusion(f32[32,64,512]{2,1,0:T(8,128)} %convert_element_type.10), kind=kLoop, calls=%fused_computation.86 | loop fusion | flops 17825792 | bytes 8388608 | tf_op jit(solution)/shard_map/add | solution.py:55
  27.0 0.1 fusion.72
  27.1 1.9 %collective-permute-start = (f32[32,4,512]{2,1,0:T(4,128)S(1)}, f32[32,4,512]{2,1,0:T(4,128)S(1)}, u32[]{:S(2)}, u32[]{:S(2)}) collective-permute-start(f32[32,4,512]{2,1,0:T(4,128)S(1)} %get-tuple-element.15), channel_id=1, source_target_pairs={{0,16},{16,32},{32,48},{48,64},{64,80},{80,96},{96,112},{112,128},... | collective-permute-start | bytes 786440 | tf_op jit(solution)/shard_map/ppermute | solution.py:23
  29.1 8.4 %collective-permute-start.1 = (f32[32,4,512]{2,1,0:T(4,128)S(1)}, f32[32,4,512]{2,1,0:T(4,128)S(1)}, u32[]{:S(2)}, u32[]{:S(2)}) collective-permute-start(f32[32,4,512]{2,1,0:T(4,128)S(1)} %get-tuple-element.16), channel_id=1, source_target_pairs={{16,0},{32,16},{48,32},{64,48},{80,64},{96,80},{112,96},{128,112},... | collective-permute-start | bytes 786440 | tf_op jit(solution)/shard_map/ppermute | solution.py:26
  37.5 2.2 %collective-permute-done = f32[32,4,512]{2,1,0:T(4,128)S(1)} collective-permute-done((f32[32,4,512]{2,1,0:T(4,128)S(1)}, f32[32,4,512]{2,1,0:T(4,128)S(1)}, u32[]{:S(2)}, u32[]{:S(2)}) %collective-permute-start) | collective-permute-done | bytes 262176 | tf_op jit(solution)/shard_map/ppermute | solution.py:23
  39.7 8.2 %collective-permute-done.1 = f32[32,4,512]{2,1,0:T(4,128)S(1)} collective-permute-done((f32[32,4,512]{2,1,0:T(4,128)S(1)}, f32[32,4,512]{2,1,0:T(4,128)S(1)}, u32[]{:S(2)}, u32[]{:S(2)}) %collective-permute-start.1) | collective-permute-done | bytes 262176 | tf_op jit(solution)/shard_map/ppermute | solution.py:26
  48.0 5.4 %fusion.23 = f32[32,64,512]{2,1,0:T(8,128)S(1)} fusion(f32[32,64,512]{2,1,0:T(8,128)S(1)} %fusion.51, f32[32,4,512]{2,1,0:T(4,128)S(1)} %collective-permute-done.1, f32[32,4,512]{2,1,0:T(4,128)S(1)} %collective-permute-done), kind=kLoop, calls=%fused_computation.58 | loop fusion | flops 26214400 | bytes 8912896 | tf_op jit(solution)/shard_map/add | solution.py:55
  53.4 0.1 fusion.71
  53.5 2.9 %collective-permute-start.2 = (f32[4,64,512]{2,1,0:T(8,128)S(1)}, f32[4,64,512]{2,1,0:T(8,128)S(1)}, u32[]{:S(2)}, u32[]{:S(2)}) collective-permute-start(f32[4,64,512]{2,1,0:T(8,128)S(1)} %get-tuple-element.13), channel_id=1, source_target_pairs={{0,1},{1,2},{2,3},{3,4},{4,5},{5,6},{6,7},{7,8},{8,9},{9,10},{10,1... | collective-permute-start | bytes 1572872 | tf_op jit(solution)/shard_map/ppermute | solution.py:23
  56.4 5.6 %collective-permute-start.3 = (f32[4,64,512]{2,1,0:T(8,128)S(1)}, f32[4,64,512]{2,1,0:T(8,128)S(1)}, u32[]{:S(2)}, u32[]{:S(2)}) collective-permute-start(f32[4,64,512]{2,1,0:T(8,128)S(1)} %get-tuple-element.14), channel_id=1, source_target_pairs={{1,0},{2,1},{3,2},{4,3},{5,4},{6,5},{7,6},{8,7},{9,8},{10,9},{11,1... | collective-permute-start | bytes 1572872 | tf_op jit(solution)/shard_map/ppermute | solution.py:26
  62.0 7.9 %collective-permute-done.2 = f32[4,64,512]{2,1,0:T(8,128)S(1)} collective-permute-done((f32[4,64,512]{2,1,0:T(8,128)S(1)}, f32[4,64,512]{2,1,0:T(8,128)S(1)}, u32[]{:S(2)}, u32[]{:S(2)}) %collective-permute-start.2) | collective-permute-done | bytes 524320 | tf_op jit(solution)/shard_map/ppermute | solution.py:23
  70.0 7.4 %collective-permute-done.3 = f32[4,64,512]{2,1,0:T(8,128)S(1)} collective-permute-done((f32[4,64,512]{2,1,0:T(8,128)S(1)}, f32[4,64,512]{2,1,0:T(8,128)S(1)}, u32[]{:S(2)}, u32[]{:S(2)}) %collective-permute-start.3) | collective-permute-done | bytes 524320 | tf_op jit(solution)/shard_map/ppermute | solution.py:26
  77.3 4.8 %fusion.3 = f32[32,64,512]{2,1,0:T(8,128)S(1)} fusion(f32[32,64,512]{2,1,0:T(8,128)S(1)} %fusion.23, f32[4,64,512]{2,1,0:T(8,128)S(1)} %collective-permute-done.3, f32[4,64,512]{2,1,0:T(8,128)S(1)} %collective-permute-done.2), kind=kLoop, calls=%fused_computation.38 | loop fusion | flops 26214400 | bytes 9437184 | tf_op jit(solution)/shard_map/add | solution.py:55
  82.1 7.1 %collective-permute-start.4 = (f32[1,64,512]{2,1,0:T(8,128)S(1)}, f32[1,64,512]{2,1,0:T(8,128)S(1)}, u32[]{:S(2)}, u32[]{:S(2)}) collective-permute-start(f32[1,64,512]{2,1,0:T(8,128)S(1)} %get-tuple-element.11), channel_id=1, source_target_pairs={{1,0},{2,1},{3,2},{4,3},{5,4},{6,5},{7,6},{8,7},{9,8},{10,9},{11,1... | collective-permute-start | bytes 393224 | tf_op jit(solution)/shard_map/ppermute | solution.py:40
  89.2 1.9 %collective-permute-start.5 = (f32[1,64,512]{2,1,0:T(8,128)S(1)}, f32[1,64,512]{2,1,0:T(8,128)S(1)}, u32[]{:S(2)}, u32[]{:S(2)}) collective-permute-start(f32[1,64,512]{2,1,0:T(8,128)S(1)} %get-tuple-element.12), channel_id=1, source_target_pairs={{0,1},{1,2},{2,3},{3,4},{4,5},{5,6},{6,7},{7,8},{8,9},{9,10},{10,1... | collective-permute-start | bytes 393224 | tf_op jit(solution)/shard_map/ppermute | solution.py:39
  91.1 0.1 fusion.69
  91.2 6.8 %collective-permute-start.6 = (f32[32,1,512]{2,1,0:T(1,128)S(1)}, f32[32,1,512]{2,1,0:T(1,128)S(1)}, u32[]{:S(2)}, u32[]{:S(2)}) collective-permute-start(f32[32,1,512]{2,1,0:T(1,128)S(1)} %get-tuple-element.9), channel_id=1, source_target_pairs={{16,0},{32,16},{48,32},{64,48},{80,64},{96,80},{112,96},{128,112},... | collective-permute-start | bytes 196616 | tf_op jit(solution)/shard_map/ppermute | solution.py:40
  98.0 2.1 %collective-permute-start.7 = (f32[32,1,512]{2,1,0:T(1,128)S(1)}, f32[32,1,512]{2,1,0:T(1,128)S(1)}, u32[]{:S(2)}, u32[]{:S(2)}) collective-permute-start(f32[32,1,512]{2,1,0:T(1,128)S(1)} %get-tuple-element.10), channel_id=1, source_target_pairs={{0,16},{16,32},{32,48},{48,64},{64,80},{80,96},{96,112},{112,128},... | collective-permute-start | bytes 196616 | tf_op jit(solution)/shard_map/ppermute | solution.py:39
  100.1 0.0 collective-permute-done.6
  100.1 8.3 %collective-permute-done.7 = f32[32,1,512]{2,1,0:T(1,128)S(1)} collective-permute-done((f32[32,1,512]{2,1,0:T(1,128)S(1)}, f32[32,1,512]{2,1,0:T(1,128)S(1)}, u32[]{:S(2)}, u32[]{:S(2)}) %collective-permute-start.7) | collective-permute-done | bytes 65568 | tf_op jit(solution)/shard_map/ppermute | solution.py:39
  108.4 0.0 collective-permute-done.4
  108.4 0.0 collective-permute-done.5
  108.4 4.3 %fusion.73 = f32[32,64,512]{2,1,0:T(8,128)S(1)} fusion(f32[32,64,512]{2,1,0:T(8,128)S(1)} %fusion.3, f32[1,64,512]{2,1,0:T(8,128)S(1)} %collective-permute-done.5, f32[1,64,512]{2,1,0:T(8,128)S(1)} %collective-permute-done.4, f32[32,1,512]{2,1,0:T(1,128)S(1)} %collective-permute-done.7, f32[32,1,512]{2,1,0:T(1,128)S(1)} %collective-permute-done.6), kind=kOutput, calls=%fused_computation.134 | output fusion | flops 67108864 | bytes 8781824 | tf_op jit(solution)/shard_map/jit(cumsum)/reduce_window_sum | solution.py:90
  112.8 14.6 %multiply_reduce_fusion.2 = (f32[64,512]{1,0:T(8,128)S(1)}, f32[64,512]{1,0:T(8,128)S(1)}, f32[64,512]{1,0:T(8,128)S(1)}, f32[64,512]{1,0:T(8,128)S(1)}) fusion(f32[32,64,512]{2,1,0:T(8,128)S(1)} %fusion.3, f32[32,64,512]{2,1,0:T(8,128)S(1)} %fusion.73, f32[1,64,512]{2,1,0:T(8,128)S(1)} %collective-permute-done.4, ...), kind=kLoop, calls=%fused_computation.118 | loop fusion | flops 68026368 | bytes 9306112 | tf_op jit(solution)/shard_map/reduce_sum | solution.py:94
  127.6 0.1 pad_maximum_fusion.10
  127.7 18.4 %all_to_all.5 = f32[4,16,4,512]{3,2,0,1:T(4,128)S(1)} all-to-all(f32[4,16,4,512]{3,2,0,1:T(4,128)S(1)} %pad_maximum_fusion.10), channel_id=1, replica_groups=mesh['img'=16,'depth'=16] {'depth'}, dimensions={1} | all-to-all | bytes 1048576 | tf_op jit(solution)/shard_map/all_to_all | solution.py:116
  146.2 0.1 fusion.67
  146.3 0.6 pad_maximum_fusion.11
  (10 shorter events, 0.3 us)
Async XLA Ops:
  27.1 12.6 %collective-permute-start = (f32[32,4,512]{2,1,0:T(4,128)S(1)}, f32[32,4,512]{2,1,0:T(4,128)S(1)}, u32[]{:S(2)}, u32[]{:S(2)}) collective-permute-start(f32[32,4,512]{2,1,0:T(4,128)S(1)} %get-tuple-element.15), channel_id=1, source_target_pairs={{0,16},{16,32},{32,48},{48,64},{64,80},{80,96},{96,112},{112,128},... | collective-permute-start | bytes 786440 | tf_op jit(solution)/shard_map/ppermute | solution.py:23
  29.1 18.9 %collective-permute-start.1 = (f32[32,4,512]{2,1,0:T(4,128)S(1)}, f32[32,4,512]{2,1,0:T(4,128)S(1)}, u32[]{:S(2)}, u32[]{:S(2)}) collective-permute-start(f32[32,4,512]{2,1,0:T(4,128)S(1)} %get-tuple-element.16), channel_id=1, source_target_pairs={{16,0},{32,16},{48,32},{64,48},{80,64},{96,80},{112,96},{128,112},... | collective-permute-start | bytes 786440 | tf_op jit(solution)/shard_map/ppermute | solution.py:26
  53.5 16.5 %collective-permute-start.2 = (f32[4,64,512]{2,1,0:T(8,128)S(1)}, f32[4,64,512]{2,1,0:T(8,128)S(1)}, u32[]{:S(2)}, u32[]{:S(2)}) collective-permute-start(f32[4,64,512]{2,1,0:T(8,128)S(1)} %get-tuple-element.13), channel_id=1, source_target_pairs={{0,1},{1,2},{2,3},{3,4},{4,5},{5,6},{6,7},{7,8},{8,9},{9,10},{10,1... | collective-permute-start | bytes 1572872 | tf_op jit(solution)/shard_map/ppermute | solution.py:23
  56.4 20.9 %collective-permute-start.3 = (f32[4,64,512]{2,1,0:T(8,128)S(1)}, f32[4,64,512]{2,1,0:T(8,128)S(1)}, u32[]{:S(2)}, u32[]{:S(2)}) collective-permute-start(f32[4,64,512]{2,1,0:T(8,128)S(1)} %get-tuple-element.14), channel_id=1, source_target_pairs={{1,0},{2,1},{3,2},{4,3},{5,4},{6,5},{7,6},{8,7},{9,8},{10,9},{11,1... | collective-permute-start | bytes 1572872 | tf_op jit(solution)/shard_map/ppermute | solution.py:26
  82.1 26.3 %collective-permute-start.4 = (f32[1,64,512]{2,1,0:T(8,128)S(1)}, f32[1,64,512]{2,1,0:T(8,128)S(1)}, u32[]{:S(2)}, u32[]{:S(2)}) collective-permute-start(f32[1,64,512]{2,1,0:T(8,128)S(1)} %get-tuple-element.11), channel_id=1, source_target_pairs={{1,0},{2,1},{3,2},{4,3},{5,4},{6,5},{7,6},{8,7},{9,8},{10,9},{11,1... | collective-permute-start | bytes 393224 | tf_op jit(solution)/shard_map/ppermute | solution.py:40
  89.2 19.2 %collective-permute-start.5 = (f32[1,64,512]{2,1,0:T(8,128)S(1)}, f32[1,64,512]{2,1,0:T(8,128)S(1)}, u32[]{:S(2)}, u32[]{:S(2)}) collective-permute-start(f32[1,64,512]{2,1,0:T(8,128)S(1)} %get-tuple-element.12), channel_id=1, source_target_pairs={{0,1},{1,2},{2,3},{3,4},{4,5},{5,6},{6,7},{7,8},{8,9},{9,10},{10,1... | collective-permute-start | bytes 393224 | tf_op jit(solution)/shard_map/ppermute | solution.py:39
  91.2 8.9 %collective-permute-start.6 = (f32[32,1,512]{2,1,0:T(1,128)S(1)}, f32[32,1,512]{2,1,0:T(1,128)S(1)}, u32[]{:S(2)}, u32[]{:S(2)}) collective-permute-start(f32[32,1,512]{2,1,0:T(1,128)S(1)} %get-tuple-element.9), channel_id=1, source_target_pairs={{16,0},{32,16},{48,32},{64,48},{80,64},{96,80},{112,96},{128,112},... | collective-permute-start | bytes 196616 | tf_op jit(solution)/shard_map/ppermute | solution.py:40
  98.0 10.4 %collective-permute-start.7 = (f32[32,1,512]{2,1,0:T(1,128)S(1)}, f32[32,1,512]{2,1,0:T(1,128)S(1)}, u32[]{:S(2)}, u32[]{:S(2)}) collective-permute-start(f32[32,1,512]{2,1,0:T(1,128)S(1)} %get-tuple-element.10), channel_id=1, source_target_pairs={{0,16},{16,32},{32,48},{48,64},{64,80},{80,96},{96,112},{112,128},... | collective-permute-start | bytes 196616 | tf_op jit(solution)/shard_map/ppermute | solution.py:39
where the time goes:
time: 150 us; the launch traced here: 147 us
  other arithmetic  57 us (38%)
  starting transfers between devices  36.8 us (25%)
  waiting for transfers between devices  34 us (23%)
  blocking collectives  18.4 us (12%)
    add x3, other arithmetic, smooth_valid(): total + gauss_taps[offset] * lax.slice_in_dim(values, offset, offset + le...  32.3 us
    all_to_all x1, blocking collectives, local(): lax.all_to_all(pieces, 'depth', split_axis=1, concat_axis=1, tiled=True)  18.4 us
    ppermute x2, waiting for transfers between devices, extended(): lax.ppermute(lax.slice_in_dim(block, 0, width, axis=dim), axis, backward)  15.6 us
    reduce_sum x1, other arithmetic, integrate(): jnp.sum(weight * red_light, 0)  14.6 us
    ppermute x2, starting transfers between devices, extended(): lax.ppermute(lax.slice_in_dim(block, 0, width, axis=dim), axis, backward)  14.1 us
    ppermute x2, starting transfers between devices, extended_2(): lax.ppermute(leading, axis, [(b, a) for a, b in up])  13.9 us
    ppermute x2, waiting for transfers between devices, extended(): lax.ppermute(lax.slice_in_dim(block, block.shape[dim] - width, None, axis...  10.2 us
    ppermute x2, waiting for transfers between devices, extended_2(): lax.ppermute(last, axis, up)  8.27 us
  transfers between devices with their start and end apart: 8, of which 5 were waited for; matrix products, arithmetic and copies ran while one was open for 0% of the time, Pallas kernels for 0%

commit v1 on v0

v1 whole, which is shorter than its diff:
```python
import math

import jax
import jax.numpy as jnp
import numpy as np
from jax import lax
from jax.experimental import pallas as pl
from jax.experimental.pallas import tpu as pltpu
from jax.sharding import PartitionSpec as P
import ml_dtypes

gauss_taps = [
    math.exp(-offset * offset / 8.0)
    / sum((math.exp(-other * other / 8.0) for other in range(-4, 5)))
    for offset in range(-4, 5)
]
MESH = pl.DeviceIdType.MESH
f32 = jnp.float32
bf16 = jnp.bfloat16


def split_taps(matrix):
    high = matrix.astype(np.float32).astype(ml_dtypes.bfloat16).astype(np.float64)
    low = (matrix - high).astype(np.float32).astype(ml_dtypes.bfloat16).astype(np.float64)
    return high, low


def column_matrix(columns):
    index = np.arange(columns)
    offset = index[:, None] - index[None, :]
    matrix = np.zeros((columns, columns))
    for k in range(-4, 5):
        matrix[offset == k] = gauss_taps[k + 4]
    high, low = split_taps(matrix)
    return np.stack([high, low]).astype(ml_dtypes.bfloat16)


def row_matrix(rows):
    target = np.full((rows + 16,), 10**6)
    target[7 : rows + 9] = np.arange(-1, rows + 1)
    source = np.full((rows + 16,), -(10**6))
    source[:rows] = np.arange(rows)
    source[rows : rows + 5] = np.arange(-5, 0)
    source[rows + 8 : rows + 13] = np.arange(rows, rows + 5)
    offset = source[None, :] - target[:, None]
    matrix = np.zeros(offset.shape)
    for k in range(-4, 5):
        matrix[offset == k] = gauss_taps[k + 4]
    high, low = split_taps(matrix)
    pad = np.zeros((rows + 16, 16))
    return np.concatenate([high, low, high, pad], axis=1).astype(np.float32)


def render_kernel(
    depth_total, img_count, depth_count,
    counts_ref, colmat_ref, rowmat_ref, out_ref,
    cnt, wcol, brow_f, brow, stage, halo, hconv, yhigh, ylow, ufield, sfield,
    pack, pack_in, partial, outbox, inbox,
    load_sem, img_send, img_recv, dep_send, dep_recv, all_send, all_recv,
):
    img = lax.axis_index("img")
    dep = lax.axis_index("depth")
    slab, rows, columns = cnt.shape
    tiles = rows // 8
    owned = rows // depth_count
    ext = rows + 16

    barrier = pltpu.get_barrier_semaphore()
    has_prev, has_next = img > 0, img < img_count - 1
    has_front, has_back = dep > 0, dep < depth_count - 1

    def greet_depth(step, carry):
        target = lax.rem(dep + step, depth_count)
        pl.semaphore_signal(barrier, inc=1, device_id=(img, target), device_id_type=MESH)
        return carry

    lax.fori_loop(1, depth_count, greet_depth, 0)
    for step in (1, img_count - 1):
        pl.semaphore_signal(
            barrier, inc=1, device_id=(lax.rem(img + step, img_count), dep), device_id_type=MESH
        )

    loads = [
        pltpu.make_async_copy(counts_ref, cnt, load_sem.at[0]),
        pltpu.make_async_copy(colmat_ref, wcol, load_sem.at[1]),
        pltpu.make_async_copy(rowmat_ref, brow_f, load_sem.at[2]),
    ]
    for load in loads:
        load.start()

    ylow[:, ext:, :] = jnp.zeros((slab, 16, columns), bf16)
    hconv[...] = jnp.zeros(hconv.shape, f32)

    @pl.when(jnp.logical_not(has_prev))
    def _():
        halo[0] = jnp.zeros(halo.shape[1:], jnp.int32)

    @pl.when(jnp.logical_not(has_next))
    def _():
        halo[1] = jnp.zeros(halo.shape[1:], jnp.int32)

    @pl.when(jnp.logical_not(has_front))
    def _():
        ufield[0:5] = jnp.zeros((5, ext, columns), f32)
        pack_in[0] = jnp.zeros(pack_in.shape[1:], f32)

    @pl.when(jnp.logical_not(has_back))
    def _():
        ufield[slab + 5 :] = jnp.zeros((5, ext, columns), f32)
        pack_in[1] = jnp.zeros(pack_in.shape[1:], f32)

    for load in loads:
        load.wait()

    for group in range(slab // 8):
        for r in range(5):
            stage[0, group, r] = cnt[group * 8 : group * 8 + 8, r, :]
            stage[1, group, r] = cnt[group * 8 : group * 8 + 8, rows - 5 + r, :]

    row_id = lax.broadcasted_iota(jnp.int32, brow_f.shape, 0)
    outside = ((row_id == 7) & (img == 0)) | ((row_id == rows + 8) & (img == img_count - 1))
    brow[...] = jnp.where(outside, 0.0, brow_f[...]).astype(bf16)

    pl.semaphore_wait(barrier, depth_count + 1)

    def img_copy(side, group):
        target = lax.rem(img + (img_count - 1 if side == 0 else 1), img_count)
        return pltpu.make_async_remote_copy(
            src_ref=stage.at[side, group],
            dst_ref=halo.at[1 - side, group],
            send_sem=img_send.at[side, group],
            recv_sem=img_recv.at[1 - side, group],
            device_id=(target, dep),
            device_id_type=MESH,
        )

    groups = slab // 8
    order = [0, groups - 1] + list(range(1, groups - 1))
    for group in order:
        for side, exists in ((0, has_prev), (1, has_next)):
            @pl.when(exists)
            def _():
                img_copy(side, group).start()

    def column_smooth(block):
        block = block.astype(f32).astype(bf16)
        return jnp.dot(block, wcol[0], preferred_element_type=f32) + jnp.dot(
            block, wcol[1], preferred_element_type=f32
        )

    def halves(value):
        high = value.astype(bf16)
        return high, (value - high.astype(f32)).astype(bf16)

    def own_columns(step, carry):
        at = pl.ds(step * 4, 4)
        smooth = column_smooth(cnt[at].reshape(4 * rows, columns))
        high, low = halves(smooth)
        yhigh[at, :rows, :] = high.reshape(4, rows, columns)
        ylow[at, :rows, :] = low.reshape(4, rows, columns)
        return carry

    lax.fori_loop(0, slab // 4, own_columns, 0)

    def rows_of_group(group):
        for side, exists in ((0, has_prev), (1, has_next)):
            @pl.when(exists)
            def _():
                img_copy(1 - side, group).wait_recv()

        for side in range(2):
            smooth = column_smooth(halo[side, group].reshape(40, columns))
            for r in range(5):
                hconv[:, side * 8 + r, :] = smooth[r * 8 : r * 8 + 8]

        def one_layer(j, carry):
            layer = group * 8 + j
            high, low = halves(hconv[j])
            yhigh[layer, rows:ext, :] = high
            ylow[layer, rows:ext, :] = low
            tall = yhigh[layer]
            field = jnp.concatenate([tall, tall, ylow[layer]], axis=0)
            ufield[layer + 5] = jnp.dot(brow[...], field, preferred_element_type=f32)
            return carry

        lax.fori_loop(0, 8, one_layer, 0)

    def depth_copies(side):
        target = lax.rem(dep + (depth_count - 1 if side == 0 else 1), depth_count)
        source = 5 if side == 0 else slab
        place = slab + 5 if side == 0 else 0
        big = pltpu.make_async_remote_copy(
            src_ref=ufield.at[source : source + 5, 8 : rows + 8, :],
            dst_ref=ufield.at[place : place + 5, 8 : rows + 8, :],
            send_sem=dep_send.at[side, 0],
            recv_sem=dep_recv.at[1 - side, 0],
            device_id=(img, target),
            device_id_type=MESH,
        )
        small = pltpu.make_async_remote_copy(
            src_ref=pack.at[side],
            dst_ref=pack_in.at[1 - side],
            send_sem=dep_send.at[side, 1],
            recv_sem=dep_recv.at[1 - side, 1],
            device_id=(img, target),
            device_id_type=MESH,
        )
        return big, small

    def send_depth(side, exists):
        first = 5 if side == 0 else slab + 1
        for j in range(4):
            pack[side, j : j + 1] = ufield[first + j, 7:8, :]
            pack[side, 4 + j : 5 + j] = ufield[first + j, rows + 8 : rows + 9, :]

        @pl.when(exists)
        def _():
            for copy in depth_copies(side):
                copy.start()

    rows_of_group(0)
    send_depth(0, has_front)
    rows_of_group(groups - 1)
    send_depth(1, has_back)
    for group in range(1, groups - 1):
        rows_of_group(group)

    def depth_smooth(low, high):
        def one_tile(tile, carry):
            r = pl.ds(pl.multiple_of(lax.div(tile, columns // 128) * 8, 8), 8)
            c = pl.ds(pl.multiple_of(lax.rem(tile, columns // 128) * 128, 128), 128)
            held = [ufield[m, r, c] for m in range(low, low + 8)]
            for m in range(low, high):
                held.append(ufield[m + 8, r, c])
                total = gauss_taps[4] * held[4]
                for k in range(4):
                    total = total + gauss_taps[k] * (held[k] + held[8 - k])
                sfield[m, r, c] = total
                held.pop(0)
            return carry

        lax.fori_loop(0, (ext // 8) * (columns // 128), one_tile, 0)

    column_id = lax.broadcasted_iota(jnp.int32, (8, columns), 1)
    at_left, at_right = column_id == 0, column_id == columns - 1

    def shade_layer(layer, tile, state):
        seen, total, red, green = state
        base = 8 + 8 * tile
        here = sfield[layer + 1, base : base + 8, :]
        dz = sfield[layer + 2, base : base + 8, :] - sfield[layer, base : base + 8, :]
        dx = sfield[layer + 1, base + 1 : base + 9, :] - sfield[layer + 1, base - 1 : base + 7, :]
        left = jnp.where(at_left, 0.0, pltpu.roll(here, 1, 1))
        right = jnp.where(at_right, 0.0, pltpu.roll(here, columns - 1, 1))
        dy = right - left
        shading = 0.55 + 0.45 * jnp.tanh(0.72 * dz + 0.9 * dx + 0.96 * dy)
        square = here * here
        bend = dz * dz + dx * dx + dy * dy
        tau = (square * pl.reciprocal(1.0 + square)) * ((1.0 + bend) * (1.5 / depth_total))
        weight = seen * (1.0 - jnp.exp(-tau))
        light = weight * shading
        centred = here - 2.5
        return (
            seen - weight,
            total + light,
            red + light * jnp.tanh(centred),
            green + light * jnp.exp(-(centred * centred)),
        )

    depth_smooth(5, slab - 3)
    zeros = jnp.zeros((8, columns), f32)
    ones = jnp.ones((8, columns), f32)
    for tile in range(tiles):
        state = lax.fori_loop(
            5,
            slab - 5,
            lambda layer, state: shade_layer(layer, tile, state),
            (ones, zeros, zeros, zeros),
        )
        for part in range(4):
            partial[part, tile] = state[part]

    for side, exists in ((1, has_back), (0, has_front)):
        @pl.when(exists)
        def _():
            for copy in depth_copies(1 - side):
                copy.wait_recv()

    for j in range(4):
        ufield[1 + j, 7:8, :] = pack_in[0, j : j + 1]
        ufield[1 + j, rows + 8 : rows + 9, :] = pack_in[0, 4 + j : 5 + j]
        ufield[slab + 5 + j, 7:8, :] = pack_in[1, j : j + 1]
        ufield[slab + 5 + j, rows + 8 : rows + 9, :] = pack_in[1, 4 + j : 5 + j]

    depth_smooth(0, 5)
    depth_smooth(slab - 3, slab + 2)

    @pl.when(jnp.logical_not(has_front))
    def _():
        sfield[0] = jnp.zeros((ext, columns), f32)

    @pl.when(jnp.logical_not(has_back))
    def _():
        sfield[slab + 1] = jnp.zeros((ext, columns), f32)

    def all_copy(target, source):
        return pltpu.make_async_remote_copy(
            src_ref=outbox.at[target],
            dst_ref=inbox.at[source],
            send_sem=all_send.at[target],
            recv_sem=all_recv.at[source],
            device_id=(img, target),
            device_id_type=MESH,
        )

    top_half = lax.broadcasted_iota(jnp.int32, (8, columns), 0) < 4
    for tile in range(tiles):
        state = lax.fori_loop(
            0, 5, lambda layer, state: shade_layer(layer, tile, state), (ones, zeros, zeros, zeros)
        )
        seen = state[0]
        state = (seen * partial[0, tile],) + tuple(
            state[part] + seen * partial[part, tile] for part in range(1, 4)
        )
        seen, total, red, green = lax.fori_loop(
            slab - 5, slab, lambda layer, state: shade_layer(layer, tile, state), state
        )
        outbox[2 * tile, 0:8] = jnp.where(top_half, total, pltpu.roll(red, 4, 0))
        outbox[2 * tile, 8:16] = jnp.where(top_half, green, pltpu.roll(seen, 4, 0))
        outbox[2 * tile + 1, 0:8] = jnp.where(top_half, pltpu.roll(total, 4, 0), red)
        outbox[2 * tile + 1, 8:16] = jnp.where(top_half, pltpu.roll(green, 4, 0), seen)
        for target in (2 * tile, 2 * tile + 1):
            @pl.when(dep != target)
            def _():
                all_copy(target, dep).start()

            @pl.when(dep == target)
            def _():
                inbox[target] = outbox[target]

    def compose(source, state):
        seen, upper, lower = state

        @pl.when(source != dep)
        def _():
            all_copy(source, source).wait_recv()

        first, second = inbox[source, 0:8, :], inbox[source, 8:16, :]
        through = jnp.where(top_half, pltpu.roll(second, 4, 0), second)
        return seen * through, upper + seen * first, lower + seen * second

    seen, upper, lower = lax.fori_loop(0, depth_count, compose, (ones, zeros, zeros))
    total, red = upper[0:4], upper[4:8]
    out_ref[0] = 0.5 * (total + red)
    out_ref[1] = lower[0:4]
    out_ref[2] = 0.5 * (total - red)
    out_ref[3] = 1.0 - seen[0:4]

    for group in range(groups):
        for side, exists in ((0, has_prev), (1, has_next)):
            @pl.when(exists)
            def _():
                img_copy(side, group).wait_send()

    for side, exists in ((0, has_front), (1, has_back)):
        @pl.when(exists)
        def _():
            for copy in depth_copies(side):
                copy.wait_send()

    def finish(target, carry):
        @pl.when(target != dep)
        def _():
            all_copy(target, target).wait_send()

        return carry

    lax.fori_loop(0, depth_count, finish, 0)


def solution(mesh):
    img_count, depth_count = mesh.shape["img"], mesh.shape["depth"]

    def local(counts):
        slab, rows, columns = counts.shape
        ext = rows + 16
        groups = slab // 8

        def body(*refs):
            render_kernel(slab * depth_count, img_count, depth_count, *refs)

        anywhere = pl.BlockSpec(memory_space=pl.ANY)
        return pl.pallas_call(
            body,
            out_shape=jax.ShapeDtypeStruct((4, rows // depth_count, columns), f32),
            in_specs=[anywhere] * 3,
            out_specs=pl.BlockSpec(memory_space=pltpu.VMEM),
            scratch_shapes=[
                pltpu.VMEM((slab, rows, columns), jnp.int32),
                pltpu.VMEM((2, columns, columns), bf16),
                pltpu.VMEM((ext, 3 * ext + 16), f32),
                pltpu.VMEM((ext, 3 * ext + 16), bf16),
                pltpu.VMEM((2, groups, 5, 8, columns), jnp.int32),
                pltpu.VMEM((2, groups, 5, 8, columns), jnp.int32),
                pltpu.VMEM((8, 16, columns), f32),
                pltpu.VMEM((slab, ext, columns), bf16),
                pltpu.VMEM((slab, ext + 16, columns), bf16),
                pltpu.VMEM((slab + 10, ext, columns), f32),
                pltpu.VMEM((slab + 2, ext, columns), f32),
                pltpu.VMEM((2, 8, columns), f32),
                pltpu.VMEM((2, 8, columns), f32),
                pltpu.VMEM((4, rows // 8, 8, columns), f32),
                pltpu.VMEM((depth_count, 16, columns), f32),
                pltpu.VMEM((depth_count, 16, columns), f32),
                pltpu.SemaphoreType.DMA((3,)),
                pltpu.SemaphoreType.DMA((2, groups)),
                pltpu.SemaphoreType.DMA((2, groups)),
                pltpu.SemaphoreType.DMA((2, 2)),
                pltpu.SemaphoreType.DMA((2, 2)),
                pltpu.SemaphoreType.DMA((depth_count,)),
                pltpu.SemaphoreType.DMA((depth_count,)),
            ],
            compiler_params=pltpu.CompilerParams(
                collective_id=0, has_side_effects=True, vmem_limit_bytes=56 << 20
            ),
        )(counts, jnp.asarray(column_matrix(columns)), jnp.asarray(row_matrix(rows)))

    return jax.shard_map(
        local,
        mesh=mesh,
        in_specs=(P("depth", "img", None),),
        out_specs=P(None, ("img", "depth"), None),
        check_vma=False,
    )
```

time: 150 us -> 76.8 us (0.51)
  the two profiles are of different devices: /device:TPU:14 before, /device:TPU:7 now
where the time goes in v1:
time: 76.8 us; the launch traced here: 76.7 us
  Pallas kernels  75.3 us (98%)
  local copies, waits for them, and re-layouts  1.38 us (2%)
    pallas_call x1, Pallas kernels, local(): pl.pallas_call(body, out_shape=jax.ShapeDtypeStruct((4, rows // depth_cou...  75.3 us

profile of v1, /device:TPU:7, one launch (start us, length us, event | category | flops | bytes accessed | tf_op | source)
XLA Modules:
  0.0 76.7 jit_solution(17401841306621421637)
XLA Ops:
  0.0 75.3 %shard_map.37 = f32[4,4,512]{2,1,0:T(4,128)} custom-call(s32[32,64,512]{2,1,0:T(8,128)} %refs_0_.1, bf16[2,512,512]{2,1,0:T(8,128)(2,1)} %constant.4.clone.refs_1_, f32[80,256]{1,0:T(8,128)} %constant.5.clone.refs_2_), custom_call_target="tpu_custom_call" | custom-call | tf_op jit(solution)/shard_map/pallas_call | solution.py:393
  75.3 1.4 %copy.5 = f32[4,4,512]{2,1,0:T(4,128)} copy(f32[4,4,512]{2,1,0:T(4,128)} %shard_map.37) | data formatting | bytes 65536

commit v2 on v1

--- a/solution.py
+++ b/solution.py
@@ -276,6 +276,7 @@
             slab - 5,
             lambda layer, state: shade_layer(layer, tile, state),
             (ones, zeros, zeros, zeros),
+            unroll=11,
         )
         for part in range(4):
             partial[part, tile] = state[part]
@@ -316,14 +317,22 @@
     top_half = lax.broadcasted_iota(jnp.int32, (8, columns), 0) < 4
     for tile in range(tiles):
         state = lax.fori_loop(
-            0, 5, lambda layer, state: shade_layer(layer, tile, state), (ones, zeros, zeros, zeros)
+            0,
+            5,
+            lambda layer, state: shade_layer(layer, tile, state),
+            (ones, zeros, zeros, zeros),
+            unroll=5,
         )
         seen = state[0]
         state = (seen * partial[0, tile],) + tuple(
             state[part] + seen * partial[part, tile] for part in range(1, 4)
         )
         seen, total, red, green = lax.fori_loop(
-            slab - 5, slab, lambda layer, state: shade_layer(layer, tile, state), state
+            slab - 5,
+            slab,
+            lambda layer, state: shade_layer(layer, tile, state),
+            state,
+            unroll=5,
         )
         outbox[2 * tile, 0:8] = jnp.where(top_half, total, pltpu.roll(red, 4, 0))
         outbox[2 * tile, 8:16] = jnp.where(top_half, green, pltpu.roll(seen, 4, 0))

time: 76.8 us -> 71 us (0.924)
  the two profiles are of different devices: /device:TPU:7 before, /device:TPU:14 now
where the time goes in v2:
time: 71 us; the launch traced here: 70.7 us
  Pallas kernels  69.3 us (98%)
  local copies, waits for them, and re-layouts  1.38 us (2%)
    pallas_call x1, Pallas kernels, local(): pl.pallas_call(body, out_shape=jax.ShapeDtypeStruct((4, rows // depth_cou...  69.3 us

profile of v2, /device:TPU:14, one launch (start us, length us, event | category | flops | bytes accessed | tf_op | source)
XLA Modules:
  0.0 70.7 jit_solution(10740025352029991054)
XLA Ops:
  0.0 69.3 %shard_map.37 = f32[4,4,512]{2,1,0:T(4,128)} custom-call(s32[32,64,512]{2,1,0:T(8,128)} %refs_0_.1, bf16[2,512,512]{2,1,0:T(8,128)(2,1)} %constant.4.clone.refs_1_, f32[80,256]{1,0:T(8,128)} %constant.5.clone.refs_2_), custom_call_target="tpu_custom_call" | custom-call | tf_op jit(solution)/shard_map/pallas_call | solution.py:402
  69.3 1.4 %copy.5 = f32[4,4,512]{2,1,0:T(4,128)} copy(f32[4,4,512]{2,1,0:T(4,128)} %shard_map.37) | data formatting | bytes 65536

commit v3 on v2

--- a/solution.py
+++ b/solution.py
@@ -17,6 +17,7 @@
 MESH = pl.DeviceIdType.MESH
 f32 = jnp.float32
 bf16 = jnp.bfloat16
+run = 4
 
 
 def split_taps(matrix):
@@ -56,7 +57,8 @@
     counts_ref, colmat_ref, rowmat_ref, out_ref,
     cnt, wcol, brow_f, brow, stage, halo, hconv, yhigh, ylow, ufield, sfield,
     pack, pack_in, partial, outbox, inbox,
-    load_sem, img_send, img_recv, dep_send, dep_recv, all_send, all_recv,
+    relay, load_sem, img_send, img_recv, dep_send, dep_recv, all_send, all_recv,
+    relay_send, relay_recv,
 ):
     img = lax.axis_index("img")
     dep = lax.axis_index("depth")
@@ -64,6 +66,8 @@
     tiles = rows // 8
     owned = rows // depth_count
     ext = rows + 16
+    chunks = dep_send.shape[1] - 1
+    chunk_rows = rows // chunks
 
     barrier = pltpu.get_barrier_semaphore()
     has_prev, has_next = img > 0, img < img_count - 1
@@ -80,10 +84,16 @@
             barrier, inc=1, device_id=(lax.rem(img + step, img_count), dep), device_id_type=MESH
         )
 
+    def load_rows(start, size, sem):
+        span = pl.ds(start, size)
+        return pltpu.make_async_copy(counts_ref.at[:, span, :], cnt.at[:, span, :], sem)
+
     loads = [
-        pltpu.make_async_copy(counts_ref, cnt, load_sem.at[0]),
-        pltpu.make_async_copy(colmat_ref, wcol, load_sem.at[1]),
-        pltpu.make_async_copy(rowmat_ref, brow_f, load_sem.at[2]),
+        load_rows(0, 8, load_sem.at[0]),
+        load_rows(rows - 8, 8, load_sem.at[1]),
+        load_rows(8, rows - 16, load_sem.at[2]),
+        pltpu.make_async_copy(colmat_ref, wcol, load_sem.at[3]),
+        pltpu.make_async_copy(rowmat_ref, brow_f, load_sem.at[4]),
     ]
     for load in loads:
         load.start()
@@ -109,17 +119,13 @@
         ufield[slab + 5 :] = jnp.zeros((5, ext, columns), f32)
         pack_in[1] = jnp.zeros(pack_in.shape[1:], f32)
 
-    for load in loads:
+    for load in loads[:2]:
         load.wait()
 
     for group in range(slab // 8):
         for r in range(5):
             stage[0, group, r] = cnt[group * 8 : group * 8 + 8, r, :]
             stage[1, group, r] = cnt[group * 8 : group * 8 + 8, rows - 5 + r, :]
-
-    row_id = lax.broadcasted_iota(jnp.int32, brow_f.shape, 0)
-    outside = ((row_id == 7) & (img == 0)) | ((row_id == rows + 8) & (img == img_count - 1))
-    brow[...] = jnp.where(outside, 0.0, brow_f[...]).astype(bf16)
 
     pl.semaphore_wait(barrier, depth_count + 1)
 
@@ -142,6 +148,13 @@
             def _():
                 img_copy(side, group).start()
 
+    for load in loads[2:]:
+        load.wait()
+
+    row_id = lax.broadcasted_iota(jnp.int32, brow_f.shape, 0)
+    outside = ((row_id == 7) & (img == 0)) | ((row_id == rows + 8) & (img == img_count - 1))
+    brow[...] = jnp.where(outside, 0.0, brow_f[...]).astype(bf16)
+
     def column_smooth(block):
         block = block.astype(f32).astype(bf16)
         return jnp.dot(block, wcol[0], preferred_element_type=f32) + jnp.dot(
@@ -185,47 +198,107 @@
 
         lax.fori_loop(0, 8, one_layer, 0)
 
-    def depth_copies(side):
-        target = lax.rem(dep + (depth_count - 1 if side == 0 else 1), depth_count)
+    def depth_target(side):
+        return lax.rem(dep + (depth_count - 1 if side == 0 else 1), depth_count)
+
+    def depth_copy(side, chunk):
         source = 5 if side == 0 else slab
         place = slab + 5 if side == 0 else 0
-        big = pltpu.make_async_remote_copy(
-            src_ref=ufield.at[source : source + 5, 8 : rows + 8, :],
-            dst_ref=ufield.at[place : place + 5, 8 : rows + 8, :],
-            send_sem=dep_send.at[side, 0],
-            recv_sem=dep_recv.at[1 - side, 0],
-            device_id=(img, target),
+        span = pl.ds(8 + chunk * chunk_rows, chunk_rows)
+        return pltpu.make_async_remote_copy(
+            src_ref=ufield.at[source : source + 5, span, :],
+            dst_ref=ufield.at[place : place + 5, span, :],
+            send_sem=dep_send.at[side, chunk],
+            recv_sem=dep_recv.at[1 - side, chunk],
+            device_id=(img, depth_target(side)),
             device_id_type=MESH,
         )
-        small = pltpu.make_async_remote_copy(
+
+    stretch = lax.div(dep, run)
+    relays = depth_count // run - 1
+
+    def goes_round(side, chunk):
+        if side == 0:
+            return has_front & (lax.rem(dep, run) == 0) & (chunk < relays + 1 - stretch)
+        return has_back & (lax.rem(dep, run) == run - 1) & (chunk <= stretch)
+
+    def round_copy(side, chunk):
+        source = 5 if side == 0 else slab
+        step = depth_count - run if side == 0 else run
+        return pltpu.make_async_remote_copy(
+            src_ref=ufield.at[source : source + 5, pl.ds(8 + chunk * chunk_rows, chunk_rows), :],
+            dst_ref=relay.at[chunk],
+            send_sem=dep_send.at[side, chunk],
+            recv_sem=relay_recv.at[chunk],
+            device_id=(img, lax.rem(dep + step, depth_count)),
+            device_id_type=MESH,
+        )
+
+    def passes_on(side, chunk):
+        if side == 0:
+            return (lax.rem(dep, run) == 0) & (chunk < relays - stretch)
+        return (lax.rem(dep, run) == run - 1) & (chunk < stretch)
+
+    def pass_copy(side, chunk):
+        place = slab + 5 if side == 0 else 0
+        step = run - 1 if side == 0 else depth_count - run + 1
+        return pltpu.make_async_remote_copy(
+            src_ref=relay.at[chunk],
+            dst_ref=ufield.at[place : place + 5, pl.ds(8 + chunk * chunk_rows, chunk_rows), :],
+            send_sem=relay_send.at[chunk],
+            recv_sem=dep_recv.at[1 - side, chunk],
+            device_id=(img, lax.rem(dep + step, depth_count)),
+            device_id_type=MESH,
+        )
+
+    def pass_on(chunk):
+        for side in range(2):
+            @pl.when(passes_on(side, chunk))
+            def _():
+                round_copy(side, chunk).wait_recv()
+                pass_copy(side, chunk).start()
+
+    def edge_copy(side):
+        return pltpu.make_async_remote_copy(
             src_ref=pack.at[side],
             dst_ref=pack_in.at[1 - side],
-            send_sem=dep_send.at[side, 1],
-            recv_sem=dep_recv.at[1 - side, 1],
-            device_id=(img, target),
+            send_sem=dep_send.at[side, chunks],
+            recv_sem=dep_recv.at[1 - side, chunks],
+            device_id=(img, depth_target(side)),
             device_id_type=MESH,
         )
-        return big, small
-
-    def send_depth(side, exists):
+
+    def pack_edges(side):
         first = 5 if side == 0 else slab + 1
         for j in range(4):
             pack[side, j : j + 1] = ufield[first + j, 7:8, :]
             pack[side, 4 + j : 5 + j] = ufield[first + j, rows + 8 : rows + 9, :]
 
-        @pl.when(exists)
-        def _():
-            for copy in depth_copies(side):
-                copy.start()
-
-    rows_of_group(0)
-    send_depth(0, has_front)
-    rows_of_group(groups - 1)
-    send_depth(1, has_back)
+    faces = ((0, has_front), (1, has_back))
+
+    for side, group in ((0, 0), (1, groups - 1)):
+        rows_of_group(group)
+        pack_edges(side)
+
+        @pl.when(faces[side][1])
+        def _():
+            edge_copy(side).start()
+
+        for chunk in range(chunks):
+            round_trip = goes_round(side, chunk)
+
+            @pl.when(round_trip)
+            def _():
+                round_copy(side, chunk).start()
+
+            @pl.when(faces[side][1] & jnp.logical_not(round_trip))
+            def _():
+                depth_copy(side, chunk).start()
+
     for group in range(1, groups - 1):
         rows_of_group(group)
 
-    def depth_smooth(low, high):
+    def depth_smooth(low, high, first, last):
         def one_tile(tile, carry):
             r = pl.ds(pl.multiple_of(lax.div(tile, columns // 128) * 8, 8), 8)
             c = pl.ds(pl.multiple_of(lax.rem(tile, columns // 128) * 128, 128), 128)
@@ -239,7 +312,8 @@
                 held.pop(0)
             return carry
 
-        lax.fori_loop(0, (ext // 8) * (columns // 128), one_tile, 0)
+        per_row = columns // 128
+        lax.fori_loop(first * per_row, last * per_row, one_tile, 0)
 
     column_id = lax.broadcasted_iota(jnp.int32, (8, columns), 1)
     at_left, at_right = column_id == 0, column_id == columns - 1
@@ -267,7 +341,7 @@
             green + light * jnp.exp(-(centred * centred)),
         )
 
-    depth_smooth(5, slab - 3)
+    depth_smooth(5, slab - 3, 0, ext // 8)
     zeros = jnp.zeros((8, columns), f32)
     ones = jnp.ones((8, columns), f32)
     for tile in range(tiles):
@@ -280,12 +354,13 @@
         )
         for part in range(4):
             partial[part, tile] = state[part]
-
-    for side, exists in ((1, has_back), (0, has_front)):
+        if tile % 2 == 0 and tile // 2 < relays:
+            pass_on(tile // 2)
+
+    for side, exists in faces:
         @pl.when(exists)
         def _():
-            for copy in depth_copies(1 - side):
-                copy.wait_recv()
+            edge_copy(1 - side).wait_recv()
 
     for j in range(4):
         ufield[1 + j, 7:8, :] = pack_in[0, j : j + 1]
@@ -293,16 +368,26 @@
         ufield[slab + 5 + j, 7:8, :] = pack_in[1, j : j + 1]
         ufield[slab + 5 + j, rows + 8 : rows + 9, :] = pack_in[1, 4 + j : 5 + j]
 
-    depth_smooth(0, 5)
-    depth_smooth(slab - 3, slab + 2)
-
-    @pl.when(jnp.logical_not(has_front))
-    def _():
-        sfield[0] = jnp.zeros((ext, columns), f32)
-
-    @pl.when(jnp.logical_not(has_back))
-    def _():
-        sfield[slab + 1] = jnp.zeros((ext, columns), f32)
+    def finish_chunk(chunk):
+        for side, exists in faces:
+            @pl.when(exists)
+            def _():
+                depth_copy(1 - side, chunk).wait_recv()
+
+        tiles_per = chunk_rows // 8
+        first = 1 + chunk * tiles_per if chunk > 0 else 0
+        last = 1 + (chunk + 1) * tiles_per if chunk < chunks - 1 else ext // 8
+        depth_smooth(0, 5, first, last)
+        depth_smooth(slab - 3, slab + 2, first, last)
+        span = slice(first * 8, last * 8)
+
+        @pl.when(jnp.logical_not(has_front))
+        def _():
+            sfield[0, span, :] = jnp.zeros((last * 8 - first * 8, columns), f32)
+
+        @pl.when(jnp.logical_not(has_back))
+        def _():
+            sfield[slab + 1, span, :] = jnp.zeros((last * 8 - first * 8, columns), f32)
 
     def all_copy(target, source):
         return pltpu.make_async_remote_copy(
@@ -315,7 +400,11 @@
         )
 
     top_half = lax.broadcasted_iota(jnp.int32, (8, columns), 0) < 4
+    ready = 0
     for tile in range(tiles):
+        while ready < chunks and ready * chunk_rows <= min(8 * tile + 8, rows - 1):
+            finish_chunk(ready)
+            ready += 1
         state = lax.fori_loop(
             0,
             5,
@@ -359,11 +448,10 @@
         return seen * through, upper + seen * first, lower + seen * second
 
     seen, upper, lower = lax.fori_loop(0, depth_count, compose, (ones, zeros, zeros))
-    total, red = upper[0:4], upper[4:8]
-    out_ref[0] = 0.5 * (total + red)
-    out_ref[1] = lower[0:4]
-    out_ref[2] = 0.5 * (total - red)
-    out_ref[3] = 1.0 - seen[0:4]
+    out_ref[0] = upper[0:4]
+    out_ref[1] = upper[4:8]
+    out_ref[2] = lower[0:4]
+    out_ref[3] = seen[0:4]
 
     for group in range(groups):
         for side, exists in ((0, has_prev), (1, has_next)):
@@ -374,8 +462,9 @@
     for side, exists in ((0, has_front), (1, has_back)):
         @pl.when(exists)
         def _():
-            for copy in depth_copies(side):
-                copy.wait_send()
+            edge_copy(side).wait_send()
+            for chunk in range(chunks):
+                depth_copy(side, chunk).wait_send()
 
     def finish(target, carry):
         @pl.when(target != dep)
@@ -385,6 +474,12 @@
         return carry
 
     lax.fori_loop(0, depth_count, finish, 0)
+
+    for chunk in range(relays):
+        for side in range(2):
+            @pl.when(passes_on(side, chunk))
+            def _():
+                pass_copy(side, chunk).wait_send()
 
 
 def solution(mesh):
@@ -399,7 +494,7 @@
             render_kernel(slab * depth_count, img_count, depth_count, *refs)
 
         anywhere = pl.BlockSpec(memory_space=pl.ANY)
-        return pl.pallas_call(
+        layers = pl.pallas_call(
             body,
             out_shape=jax.ShapeDtypeStruct((4, rows // depth_count, columns), f32),
             in_specs=[anywhere] * 3,
@@ -421,18 +516,25 @@
                 pltpu.VMEM((4, rows // 8, 8, columns), f32),
                 pltpu.VMEM((depth_count, 16, columns), f32),
                 pltpu.VMEM((depth_count, 16, columns), f32),
-                pltpu.SemaphoreType.DMA((3,)),
+                pltpu.VMEM((depth_count // run, 5, rows * run // depth_count, columns), f32),
+                pltpu.SemaphoreType.DMA((5,)),
                 pltpu.SemaphoreType.DMA((2, groups)),
                 pltpu.SemaphoreType.DMA((2, groups)),
-                pltpu.SemaphoreType.DMA((2, 2)),
-                pltpu.SemaphoreType.DMA((2, 2)),
+                pltpu.SemaphoreType.DMA((2, depth_count // run + 1)),
+                pltpu.SemaphoreType.DMA((2, depth_count // run + 1)),
                 pltpu.SemaphoreType.DMA((depth_count,)),
                 pltpu.SemaphoreType.DMA((depth_count,)),
+                pltpu.SemaphoreType.DMA((depth_count // run,)),
+                pltpu.SemaphoreType.DMA((depth_count // run,)),
             ],
             compiler_params=pltpu.CompilerParams(
                 collective_id=0, has_side_effects=True, vmem_limit_bytes=56 << 20
             ),
         )(counts, jnp.asarray(column_matrix(columns)), jnp.asarray(row_matrix(rows)))
+        total, red, green, seen = (layers[part : part + 1] for part in range(4))
+        return jnp.concatenate(
+            [0.5 * (total + red), green, 0.5 * (total - red), 1.0 - seen], axis=0
+        )
 
     return jax.shard_map(
         local,

time: 71 us -> 64.2 us (0.904)
  Pallas kernels: 69.3 us -> 62.7 us
  other arithmetic: 0 us -> 1.38 us
  local copies, waits for them, and re-layouts: 1.38 us -> 0 us
    pallas_call x1, Pallas kernels: 69.3 us -> 62.7 us  [local(): pl.pallas_call(body, out_shape=jax.ShapeDtypeStruct((4, rows // depth_cou...]
    unnamed x1 -> x0, local copies, waits for them, and re-layouts: 1.38 us -> none
    mul x0 -> x1, other arithmetic: none -> 0.76 us  [local(): 0.5 * (total + red)]
where the time goes in v3:
time: 64.2 us; the launch traced here: 64.1 us
  Pallas kernels  62.7 us (98%)
  other arithmetic  1.38 us (2%)
    pallas_call x1, Pallas kernels, local(): pl.pallas_call(body, out_shape=jax.ShapeDtypeStruct((4, rows // depth_cou...  62.7 us

profile of v3, /device:TPU:14, one launch (start us, length us, event | category | flops | bytes accessed | tf_op | source)
XLA Modules:
  0.0 64.1 jit_solution(14869085169174075597)
XLA Ops:
  0.0 62.7 %shard_map.37 = f32[4,4,512]{2,1,0:T(4,128)} custom-call(s32[32,64,512]{2,1,0:T(8,128)} %refs_0_.1, bf16[2,512,512]{2,1,0:T(8,128)(2,1)} %constant.8.clone.refs_1_, f32[80,256]{1,0:T(8,128)} %constant.9.clone.refs_2_), custom_call_target="tpu_custom_call" | custom-call | tf_op jit(solution)/shard_map/pallas_call | solution.py:497
  62.7 0.8 %add_multiply_fusion = (f32[1,4,512]{2,1,0:T(4,128)S(1)}, f32[1,4,512]{2,1,0:T(4,128)S(1)}, f32[1,4,512]{2,1,0:T(4,128)S(1)}, f32[1,4,512]{2,1,0:T(4,128)S(1)}) fusion(f32[4,4,512]{2,1,0:T(4,128)} %shard_map.37), kind=kLoop, calls=%fused_computation.3 | loop fusion | flops 10240 | bytes 65536 | tf_op jit(solution)/shard_map/mul | solution.py:536
  63.5 0.6 pad_maximum_fusion

commit v4 on v3

--- a/solution.py
+++ b/solution.py
@@ -18,6 +18,7 @@
 f32 = jnp.float32
 bf16 = jnp.bfloat16
 run = 4
+img_run = 4
 
 
 def split_taps(matrix):
@@ -58,7 +59,7 @@
     cnt, wcol, brow_f, brow, stage, halo, hconv, yhigh, ylow, ufield, sfield,
     pack, pack_in, partial, outbox, inbox,
     relay, load_sem, img_send, img_recv, dep_send, dep_recv, all_send, all_recv,
-    relay_send, relay_recv,
+    relay_send, relay_recv, img_relay, img_relay_send, img_relay_recv,
 ):
     img = lax.axis_index("img")
     dep = lax.axis_index("depth")
@@ -79,7 +80,10 @@
         return carry
 
     lax.fori_loop(1, depth_count, greet_depth, 0)
-    for step in (1, img_count - 1):
+    img_partners = [
+        step for near in (1, img_run - 1, img_run) for step in (near, img_count - near)
+    ]
+    for step in img_partners:
         pl.semaphore_signal(
             barrier, inc=1, device_id=(lax.rem(img + step, img_count), dep), device_id_type=MESH
         )
@@ -127,7 +131,7 @@
             stage[0, group, r] = cnt[group * 8 : group * 8 + 8, r, :]
             stage[1, group, r] = cnt[group * 8 : group * 8 + 8, rows - 5 + r, :]
 
-    pl.semaphore_wait(barrier, depth_count + 1)
+    pl.semaphore_wait(barrier, depth_count - 1 + len(img_partners))
 
     def img_copy(side, group):
         target = lax.rem(img + (img_count - 1 if side == 0 else 1), img_count)
@@ -140,13 +144,50 @@
             device_id_type=MESH,
         )
 
+    def goes_round_img(side, group):
+        if group not in round_groups:
+            return False
+        return img == (img_run if side == 0 else img_count - 1 - img_run)
+
+    def round_img_copy(side, group):
+        return pltpu.make_async_remote_copy(
+            src_ref=stage.at[side, group],
+            dst_ref=img_relay.at[group - round_groups[0]],
+            send_sem=img_send.at[side, group],
+            recv_sem=img_relay_recv.at[group - round_groups[0]],
+            device_id=(lax.rem(img + (img_count - img_run if side == 0 else img_run), img_count), dep),
+            device_id_type=MESH,
+        )
+
+    def pass_img_copy(side, group):
+        step = img_run - 1 if side == 0 else img_count - img_run + 1
+        return pltpu.make_async_remote_copy(
+            src_ref=img_relay.at[group - round_groups[0]],
+            dst_ref=halo.at[1 - side, group],
+            send_sem=img_relay_send.at[group - round_groups[0]],
+            recv_sem=img_recv.at[1 - side, group],
+            device_id=(lax.rem(img + step, img_count), dep),
+            device_id_type=MESH,
+        )
+
     groups = slab // 8
+    round_groups = (2,)
+    img_relays = ((0, img == 0), (1, img == img_count - 1))
     order = [0, groups - 1] + list(range(1, groups - 1))
+    for side in range(2):
+        for group in round_groups:
+            @pl.when(goes_round_img(side, group))
+            def _():
+                round_img_copy(side, group).start()
+
     for group in order:
         for side, exists in ((0, has_prev), (1, has_next)):
-            @pl.when(exists)
+            round_trip = goes_round_img(side, group)
+
+            @pl.when(exists & jnp.logical_not(round_trip))
             def _():
                 img_copy(side, group).start()
+
 
     for load in loads[2:]:
         load.wait()
@@ -174,6 +215,13 @@
         return carry
 
     lax.fori_loop(0, slab // 4, own_columns, 0)
+
+    for side, relaying in img_relays:
+        @pl.when(relaying)
+        def _():
+            for group in round_groups:
+                round_img_copy(side, group).wait_recv()
+                pass_img_copy(side, group).start()
 
     def rows_of_group(group):
         for side, exists in ((0, has_prev), (1, has_next)):
@@ -317,13 +365,20 @@
 
     column_id = lax.broadcasted_iota(jnp.int32, (8, columns), 1)
     at_left, at_right = column_id == 0, column_id == columns - 1
+    row_in_tile = lax.broadcasted_iota(jnp.int32, (8, columns), 0)
+    is_first_row, is_last_row = row_in_tile == 0, row_in_tile == 7
 
     def shade_layer(layer, tile, state):
         seen, total, red, green = state
-        base = 8 + 8 * tile
-        here = sfield[layer + 1, base : base + 8, :]
-        dz = sfield[layer + 2, base : base + 8, :] - sfield[layer, base : base + 8, :]
-        dx = sfield[layer + 1, base + 1 : base + 9, :] - sfield[layer + 1, base - 1 : base + 7, :]
+        base = pl.multiple_of(8 + 8 * tile, 8)
+        span = pl.ds(base, 8)
+        here = sfield[layer + 1, span, :]
+        dz = sfield[layer + 2, span, :] - sfield[layer, span, :]
+        above = sfield[layer + 1, pl.ds(pl.multiple_of(8 * tile, 8), 8), :]
+        below = sfield[layer + 1, pl.ds(pl.multiple_of(16 + 8 * tile, 8), 8), :]
+        before = pltpu.roll(jnp.where(is_last_row, above, here), 1, 0)
+        after = pltpu.roll(jnp.where(is_first_row, below, here), 7, 0)
+        dx = after - before
         left = jnp.where(at_left, 0.0, pltpu.roll(here, 1, 1))
         right = jnp.where(at_right, 0.0, pltpu.roll(here, columns - 1, 1))
         dy = right - left
@@ -344,18 +399,25 @@
     depth_smooth(5, slab - 3, 0, ext // 8)
     zeros = jnp.zeros((8, columns), f32)
     ones = jnp.ones((8, columns), f32)
-    for tile in range(tiles):
-        state = lax.fori_loop(
-            5,
-            slab - 5,
+    def shade_layers(first, last, tile, state):
+        return lax.fori_loop(
+            first,
+            last,
             lambda layer, state: shade_layer(layer, tile, state),
-            (ones, zeros, zeros, zeros),
-            unroll=11,
-        )
+            state,
+            unroll=min(last - first, 11),
+        )
+
+    def inner_tile(tile, carry):
+        state = shade_layers(5, slab - 5, tile, (ones, zeros, zeros, zeros))
         for part in range(4):
             partial[part, tile] = state[part]
-        if tile % 2 == 0 and tile // 2 < relays:
-            pass_on(tile // 2)
+        return carry
+
+    for chunk in range(relays):
+        lax.fori_loop(chunk * 2, chunk * 2 + 2, inner_tile, 0)
+        pass_on(chunk)
+    lax.fori_loop(relays * 2, tiles, inner_tile, 0)
 
     for side, exists in faces:
         @pl.when(exists)
@@ -399,30 +461,14 @@
             device_id_type=MESH,
         )
 
-    top_half = lax.broadcasted_iota(jnp.int32, (8, columns), 0) < 4
-    ready = 0
-    for tile in range(tiles):
-        while ready < chunks and ready * chunk_rows <= min(8 * tile + 8, rows - 1):
-            finish_chunk(ready)
-            ready += 1
-        state = lax.fori_loop(
-            0,
-            5,
-            lambda layer, state: shade_layer(layer, tile, state),
-            (ones, zeros, zeros, zeros),
-            unroll=5,
-        )
+    top_half = row_in_tile < 4
+    def outer_tile(tile, carry):
+        state = shade_layers(0, 5, tile, (ones, zeros, zeros, zeros))
         seen = state[0]
         state = (seen * partial[0, tile],) + tuple(
             state[part] + seen * partial[part, tile] for part in range(1, 4)
         )
-        seen, total, red, green = lax.fori_loop(
-            slab - 5,
-            slab,
-            lambda layer, state: shade_layer(layer, tile, state),
-            state,
-            unroll=5,
-        )
+        seen, total, red, green = shade_layers(slab - 5, slab, tile, state)
         outbox[2 * tile, 0:8] = jnp.where(top_half, total, pltpu.roll(red, 4, 0))
         outbox[2 * tile, 8:16] = jnp.where(top_half, green, pltpu.roll(seen, 4, 0))
         outbox[2 * tile + 1, 0:8] = jnp.where(top_half, pltpu.roll(total, 4, 0), red)
@@ -436,6 +482,15 @@
             def _():
                 inbox[target] = outbox[target]
 
+        return carry
+
+    begun = 0
+    for chunk in range(chunks):
+        finish_chunk(chunk)
+        done = tiles if chunk == chunks - 1 else (chunk + 1) * (chunk_rows // 8) - 1
+        lax.fori_loop(begun, done, outer_tile, 0)
+        begun = done
+
     def compose(source, state):
         seen, upper, lower = state
 
@@ -448,10 +503,11 @@
         return seen * through, upper + seen * first, lower + seen * second
 
     seen, upper, lower = lax.fori_loop(0, depth_count, compose, (ones, zeros, zeros))
-    out_ref[0] = upper[0:4]
-    out_ref[1] = upper[4:8]
-    out_ref[2] = lower[0:4]
-    out_ref[3] = seen[0:4]
+    total, red = upper[0:4], upper[4:8]
+    out_ref[0] = -0.5 * (total + red)
+    out_ref[1] = -lower[0:4]
+    out_ref[2] = -0.5 * (total - red)
+    out_ref[3] = seen[0:4] - 1.0
 
     for group in range(groups):
         for side, exists in ((0, has_prev), (1, has_next)):
@@ -480,6 +536,12 @@
             @pl.when(passes_on(side, chunk))
             def _():
                 pass_copy(side, chunk).wait_send()
+
+    for side, relaying in img_relays:
+        @pl.when(relaying)
+        def _():
+            for group in round_groups:
+                pass_img_copy(side, group).wait_send()
 
 
 def solution(mesh):
@@ -526,15 +588,15 @@
                 pltpu.SemaphoreType.DMA((depth_count,)),
                 pltpu.SemaphoreType.DMA((depth_count // run,)),
                 pltpu.SemaphoreType.DMA((depth_count // run,)),
+                pltpu.VMEM((2, 5, 8, columns), jnp.int32),
+                pltpu.SemaphoreType.DMA((2,)),
+                pltpu.SemaphoreType.DMA((2,)),
             ],
             compiler_params=pltpu.CompilerParams(
                 collective_id=0, has_side_effects=True, vmem_limit_bytes=56 << 20
             ),
         )(counts, jnp.asarray(column_matrix(columns)), jnp.asarray(row_matrix(rows)))
-        total, red, green, seen = (layers[part : part + 1] for part in range(4))
-        return jnp.concatenate(
-            [0.5 * (total + red), green, 0.5 * (total - red), 1.0 - seen], axis=0
-        )
+        return -layers
 
     return jax.shard_map(
         local,

time: 64.2 us -> 63.4 us (0.988)
  Pallas kernels: 62.7 us -> 61.9 us
    neg x0 -> x1, other arithmetic: none -> 1.38 us  [local(): return -layers]
    pallas_call x1, Pallas kernels: 62.7 us -> 61.9 us  [local(): pl.pallas_call(body, out_shape=jax.ShapeDtypeStruct((4, rows // depth_cou...]
    mul x1 -> x0, other arithmetic: 0.76 us -> none  [local(): 0.5 * (total + red)]
where the time goes in v4:
time: 63.4 us; the launch traced here: 63.3 us
  Pallas kernels  61.9 us (98%)
  other arithmetic  1.38 us (2%)
    pallas_call x1, Pallas kernels, local(): pl.pallas_call(body, out_shape=jax.ShapeDtypeStruct((4, rows // depth_cou...  61.9 us
    neg x1, other arithmetic, local(): return -layers  1.38 us

profile of v4, /device:TPU:14, one launch (start us, length us, event | category | flops | bytes accessed | tf_op | source)
XLA Modules:
  0.0 63.3 jit_solution(9053071932518570205)
XLA Ops:
  0.0 61.9 %shard_map.37 = f32[4,4,512]{2,1,0:T(4,128)} custom-call(s32[32,64,512]{2,1,0:T(8,128)} %refs_0_.1, bf16[2,512,512]{2,1,0:T(8,128)(2,1)} %constant.4.clone.refs_1_, f32[80,256]{1,0:T(8,128)} %constant.5.clone.refs_2_), custom_call_target="tpu_custom_call" | custom-call | tf_op jit(solution)/shard_map/pallas_call | solution.py:559
  61.9 1.4 %neg.3 = f32[4,4,512]{2,1,0:T(4,128)} negate(f32[4,4,512]{2,1,0:T(4,128)} %shard_map.37) | non-fusion elementwise | flops 8192 | bytes 65536 | tf_op jit(solution)/shard_map/neg | solution.py:599

commit v5 on v4

--- a/solution.py
+++ b/solution.py
@@ -214,16 +214,16 @@
         ylow[at, :rows, :] = low.reshape(4, rows, columns)
         return carry
 
-    lax.fori_loop(0, slab // 4, own_columns, 0)
-
-    for side, relaying in img_relays:
-        @pl.when(relaying)
-        def _():
-            for group in round_groups:
-                round_img_copy(side, group).wait_recv()
-                pass_img_copy(side, group).start()
+    def pass_rows():
+        for side, relaying in img_relays:
+            @pl.when(relaying)
+            def _():
+                for group in round_groups:
+                    round_img_copy(side, group).wait_recv()
+                    pass_img_copy(side, group).start()
 
     def rows_of_group(group):
+        lax.fori_loop(group * 2, group * 2 + 2, own_columns, 0)
         for side, exists in ((0, has_prev), (1, has_next)):
             @pl.when(exists)
             def _():
@@ -326,6 +326,8 @@
 
     for side, group in ((0, 0), (1, groups - 1)):
         rows_of_group(group)
+        if side == 0:
+            pass_rows()
         pack_edges(side)
 
         @pl.when(faces[side][1])
@@ -430,26 +432,24 @@
         ufield[slab + 5 + j, 7:8, :] = pack_in[1, j : j + 1]
         ufield[slab + 5 + j, rows + 8 : rows + 9, :] = pack_in[1, 4 + j : 5 + j]
 
-    def finish_chunk(chunk):
-        for side, exists in faces:
-            @pl.when(exists)
-            def _():
-                depth_copy(1 - side, chunk).wait_recv()
+    def finish_chunk(side, chunk):
+        @pl.when(faces[side][1])
+        def _():
+            depth_copy(1 - side, chunk).wait_recv()
 
         tiles_per = chunk_rows // 8
         first = 1 + chunk * tiles_per if chunk > 0 else 0
         last = 1 + (chunk + 1) * tiles_per if chunk < chunks - 1 else ext // 8
-        depth_smooth(0, 5, first, last)
-        depth_smooth(slab - 3, slab + 2, first, last)
         span = slice(first * 8, last * 8)
-
-        @pl.when(jnp.logical_not(has_front))
-        def _():
-            sfield[0, span, :] = jnp.zeros((last * 8 - first * 8, columns), f32)
-
-        @pl.when(jnp.logical_not(has_back))
-        def _():
-            sfield[slab + 1, span, :] = jnp.zeros((last * 8 - first * 8, columns), f32)
+        if side == 0:
+            depth_smooth(0, 5, first, last)
+        else:
+            depth_smooth(slab - 3, slab + 2, first, last)
+
+        @pl.when(jnp.logical_not(faces[side][1]))
+        def _():
+            beyond = 0 if side == 0 else slab + 1
+            sfield[beyond, span, :] = jnp.zeros((last * 8 - first * 8, columns), f32)
 
     def all_copy(target, source):
         return pltpu.make_async_remote_copy(
@@ -462,13 +462,20 @@
         )
 
     top_half = row_in_tile < 4
+    def back_tile(tile, carry):
+        state = shade_layers(slab - 5, slab, tile, (ones, zeros, zeros, zeros))
+        seen = partial[0, tile]
+        for part in range(1, 4):
+            partial[part, tile] = partial[part, tile] + seen * state[part]
+        partial[0, tile] = seen * state[0]
+        return carry
+
     def outer_tile(tile, carry):
         state = shade_layers(0, 5, tile, (ones, zeros, zeros, zeros))
-        seen = state[0]
-        state = (seen * partial[0, tile],) + tuple(
-            state[part] + seen * partial[part, tile] for part in range(1, 4)
-        )
-        seen, total, red, green = shade_layers(slab - 5, slab, tile, state)
+        total, red, green = (
+            state[part] + state[0] * partial[part, tile] for part in range(1, 4)
+        )
+        seen = state[0] * partial[0, tile]
         outbox[2 * tile, 0:8] = jnp.where(top_half, total, pltpu.roll(red, 4, 0))
         outbox[2 * tile, 8:16] = jnp.where(top_half, green, pltpu.roll(seen, 4, 0))
         outbox[2 * tile + 1, 0:8] = jnp.where(top_half, pltpu.roll(total, 4, 0), red)
@@ -486,8 +493,10 @@
 
     begun = 0
     for chunk in range(chunks):
-        finish_chunk(chunk)
         done = tiles if chunk == chunks - 1 else (chunk + 1) * (chunk_rows // 8) - 1
+        finish_chunk(1, chunk)
+        lax.fori_loop(begun, done, back_tile, 0)
+        finish_chunk(0, chunk)
         lax.fori_loop(begun, done, outer_tile, 0)
         begun = done
 

time: 63.4 us -> 63.4 us (level)
  no operation moved by 1% of the time
where the time goes in v5:
time: 63.4 us; the launch traced here: 63.3 us
  Pallas kernels  61.9 us (98%)
  other arithmetic  1.38 us (2%)
    pallas_call x1, Pallas kernels, local(): pl.pallas_call(body, out_shape=jax.ShapeDtypeStruct((4, rows // depth_cou...  61.9 us
    neg x1, other arithmetic, local(): return -layers  1.38 us

profile of v5, /device:TPU:14, one launch (start us, length us, event | category | flops | bytes accessed | tf_op | source)
XLA Modules:
  0.0 63.3 jit_solution(4761456775192609853)
XLA Ops:
  0.0 61.9 %shard_map.37 = f32[4,4,512]{2,1,0:T(4,128)} custom-call(s32[32,64,512]{2,1,0:T(8,128)} %refs_0_.1, bf16[2,512,512]{2,1,0:T(8,128)(2,1)} %constant.4.clone.refs_1_, f32[80,256]{1,0:T(8,128)} %constant.5.clone.refs_2_), custom_call_target="tpu_custom_call" | custom-call | tf_op jit(solution)/shard_map/pallas_call | solution.py:568
  61.9 1.4 %neg.3 = f32[4,4,512]{2,1,0:T(4,128)} negate(f32[4,4,512]{2,1,0:T(4,128)} %shard_map.37) | non-fusion elementwise | flops 8192 | bytes 65536 | tf_op jit(solution)/shard_map/neg | solution.py:608

commit v6 on v5

--- a/solution.py
+++ b/solution.py
@@ -398,6 +398,7 @@
             green + light * jnp.exp(-(centred * centred)),
         )
 
+    pass_on(0)
     depth_smooth(5, slab - 3, 0, ext // 8)
     zeros = jnp.zeros((8, columns), f32)
     ones = jnp.ones((8, columns), f32)
@@ -416,10 +417,10 @@
             partial[part, tile] = state[part]
         return carry
 
-    for chunk in range(relays):
-        lax.fori_loop(chunk * 2, chunk * 2 + 2, inner_tile, 0)
-        pass_on(chunk)
-    lax.fori_loop(relays * 2, tiles, inner_tile, 0)
+    pass_on(1)
+    lax.fori_loop(0, 3, inner_tile, 0)
+    pass_on(2)
+    lax.fori_loop(3, tiles, inner_tile, 0)
 
     for side, exists in faces:
         @pl.when(exists)

time: 63.4 us -> 63.4 us (level)
  no operation moved by 1% of the time
where the time goes in v6:
time: 63.4 us; the launch traced here: 63.3 us
  Pallas kernels  61.9 us (98%)
  other arithmetic  1.38 us (2%)
    pallas_call x1, Pallas kernels, local(): pl.pallas_call(body, out_shape=jax.ShapeDtypeStruct((4, rows // depth_cou...  61.9 us
    neg x1, other arithmetic, local(): return -layers  1.38 us

profile of v6, /device:TPU:14, one launch (start us, length us, event | category | flops | bytes accessed | tf_op | source)
XLA Modules:
  0.0 63.3 jit_solution(11153513342521151992)
XLA Ops:
  0.0 61.9 %shard_map.37 = f32[4,4,512]{2,1,0:T(4,128)} custom-call(s32[32,64,512]{2,1,0:T(8,128)} %refs_0_.1, bf16[2,512,512]{2,1,0:T(8,128)(2,1)} %constant.4.clone.refs_1_, f32[80,256]{1,0:T(8,128)} %constant.5.clone.refs_2_), custom_call_target="tpu_custom_call" | custom-call | tf_op jit(solution)/shard_map/pallas_call | solution.py:569
  61.9 1.4 %neg.3 = f32[4,4,512]{2,1,0:T(4,128)} negate(f32[4,4,512]{2,1,0:T(4,128)} %shard_map.37) | non-fusion elementwise | flops 8192 | bytes 65536 | tf_op jit(solution)/shard_map/neg | solution.py:609
